TPU v7x, 32 devices: a whole 2x2x4 slice. The times are simulated.
32 devices in a mesh: cuts: 2 (over x), mode: 8 (over z, y), branch: 2 (over core).
Axes of the slice: x: 2, y: 2, z: 4, core: 2. Of those that a mesh axis runs over, the one named last changes fastest.
Arguments:
- leaves: bfloat16 [8, 2, 32, 512, 512], P('branch', None, ('cuts', 'mode')), parts along dimension 2, may hold values from -0.1875 to 0.1875
- join_order: int32 [7], replicated, may hold values from 0 to 1
- slice_values: int32 [32], P(('cuts', 'mode')), parts along dimension 0, may hold values from 0 to 1
- boundary: bfloat16 [2, 2, 512, 512], replicated, may hold values from -4 to 4
Outputs:
- amplitudes: float32 [2, 32, 512, 512], P(None, ('cuts', 'mode'), 'branch'), parts along dimension 1
There are 2 independent parts, one for each index of `cuts`. A program takes and returns all parts, laid end to end along the dimension named above; an argument that names none is the same for every part. Nothing has to cross between parts.
Inputs may be any that keep to these rules, and one draw needn't show every extreme that they name: `join_order`: 1 puts the second operand of the join on the left.
All inputs are finite; a program needn't handle non-finite values.
Results may differ from a plain program's by a relative error of at most 0.0076.
Values may be sent and summed in bfloat16 or wider, within the bound.
A program may use at most 64 MiB of HBM per device.

v0:
```python
import jax
import jax.numpy as jnp
from jax import lax
from jax.sharding import PartitionSpec as P


def from_partner(value, axis, bit):
    mask = 2**bit
    pairs = [(source, source ^ mask) for source in range(lax.axis_size(axis))]
    return lax.ppermute(value, axis, pairs)


def complex_sums(left_op, right_op):
    spec = "bij,bjk->bik"
    real_part = jnp.einsum(
        spec, left_op[0], right_op[0], preferred_element_type=jnp.float32
    ) - jnp.einsum(spec, left_op[1], right_op[1], preferred_element_type=jnp.float32)
    imag_part = jnp.einsum(
        spec, left_op[0], right_op[1], preferred_element_type=jnp.float32
    ) + jnp.einsum(spec, left_op[1], right_op[0], preferred_element_type=jnp.float32)
    return jnp.stack([real_part, imag_part])


def complex_product(left_op, right_op):
    return complex_sums(left_op, right_op).astype(jnp.bfloat16)


def join_pair(left_op, right_op, swapped):
    return lax.cond(
        swapped == 1,
        lambda: complex_product(right_op, left_op),
        lambda: complex_product(left_op, right_op),
    )


def split_rows(tensor, blocks):
    shape = tensor.shape
    return tensor.reshape(shape[0], shape[1], blocks, shape[2] // blocks, shape[3])


def merge_rows(tensor):
    shape = tensor.shape
    width = shape[4]
    total_rows = shape[1] * shape[2] * shape[3]
    return tensor.reshape(shape[0], total_rows // width, width, width)


def per_device(leaves, join_order, slice_values, boundary):
    blocks = lax.axis_size("mode")
    branch_index = lax.axis_index("branch")
    base_index = 2 * branch_index
    first_pair = join_pair(leaves[0], leaves[1], join_order[base_index])
    second_pair = join_pair(leaves[2], leaves[3], join_order[base_index + 1])
    first_pair, second_pair = (
        lax.all_to_all(
            split_rows(first_pair, blocks), "mode", split_axis=2, concat_axis=1, tiled=True
        ),
        lax.all_to_all(
            split_rows(second_pair, blocks), "mode", split_axis=2, concat_axis=1, tiled=True
        ),
    )
    first_pair = merge_rows(first_pair)
    second_pair = merge_rows(second_pair)
    middle = join_pair(first_pair, second_pair, join_order[4 + branch_index])
    middle = merge_rows(
        lax.all_to_all(split_rows(middle, blocks), "mode", split_axis=2, concat_axis=1, tiled=True)
    )
    width = middle.shape[3]
    half_rows = width // 2
    chosen = jnp.where(
        slice_values[None, :, None, None] == 1, boundary[1][:, None], boundary[0][:, None]
    )
    top_order = join_order[-1]
    partner = from_partner(middle, "branch", 0)
    is_first = branch_index == 0
    upper = jnp.where(is_first, middle, partner)
    lower = jnp.where(is_first, partner, middle)
    leading = jnp.where(top_order == 1, lower, upper)
    trailing = jnp.where(top_order == 1, upper, lower)
    leading = lax.dynamic_slice_in_dim(leading, branch_index * half_rows, half_rows, 2)
    top_half = complex_product(leading, trailing)
    amplitudes = complex_sums(top_half, chosen)
    return amplitudes


def solution(mesh):
    in_specs = (P("branch", None, ("cuts", "mode"), None, None), P(), P(("cuts", "mode")), P())
    out_specs = P(None, ("cuts", "mode"), "branch", None)
    return jax.shard_map(
        per_device, mesh=mesh, in_specs=in_specs, out_specs=out_specs, check_vma=False
    )
```

profile of v0, /device:TPU:13, one launch (start us, length us, event | category | flops | bytes accessed | tf_op | source)
XLA Modules:
  0.0 192.8 jit_solution(156778789101351986)
XLA Ops:
  0.0 5.7 %slice_bitcast_fusion = (bf16[2,2,512,512]{3,2,1,0:T(8,128)(2,1)}, bf16[2,2,512,512]{3,2,1,0:T(8,128)(2,1)S(1)}, bf16[2,2,512,512]{3,2,1,0:T(8,128)(2,1)}, bf16[2,2,512,512]{3,2,1,0:T(8,128)(2,1)}) fusion(bf16[4,2,2,512,512]{4,3,2,1,0:T(8,128)(2,1)} %param.10), kind=kLoop, calls=%fused_computation.127 | loop fusion | bytes 16777216 | tf_op jit(solution)/shard_map/squeeze | solution.py:53
  7.0 6.6 %conditional.7 = (bf16[2,2,512,512]{3,2,1,0:T(8,128)(2,1)}) conditional(s32[]{:T(128)} %bitcast.45, (bf16[2,2,512,512]{3,2,1,0:T(8,128)(2,1)}, bf16[2,2,512,512]{3,2,1,0:T(8,128)(2,1)}) %tuple.34, (bf16[2,2,512,512]{3,2,1,0:T(8,128)(2,1)}, bf16[2,2,512,512]{3,2,1,0:T(8,128)(2,1)}) %tuple.35), branch_computations={%region_2.0_spmd, %region_3.0_spmd} | conditional | flops 2150629376 | bytes 39845952
  7.1 2.4 %fusion.36 = f32[2,512,512]{2,1,0:T(8,128)S(1)} fusion(bf16[2,2,512,512]{3,2,1,0:T(8,128)(2,1)} %get-tuple-element.49, bf16[2,2,512,512]{3,2,1,0:T(8,128)(2,1)} %get-tuple-element.48), kind=kOutput, calls=%fused_computation.45 | convolution fusion | flops 536870912 | bytes 4194304 | tf_op jit(solution)/shard_map/cond/branch_0_fun/bij,bjk->bik/dot_general | solution.py:18
  9.9 0.7 add_bitcast_fusion.2
  10.6 0.7 fusion.42
  11.3 0.7 subtract_bitcast_fusion.2
  12.1 1.6 pad_maximum_fusion.2
  13.6 3.2 %copy.11 = bf16[2,2,8,64,512]{4,3,1,0,2:T(8,128)(2,1)} copy(bf16[2,2,8,64,512]{4,3,2,1,0:T(8,128)(2,1)} %bitcast.213) | data formatting | bytes 4194304 | tf_op jit(solution)/shard_map/reshape | solution.py:38
  16.8 5.7 %all-to-all-start.1 = ((bf16[2,2,8,64,512]{4,3,1,0,2:T(8,128)(2,1)}), bf16[2,2,8,64,512]{4,3,1,0,2:T(8,128)(2,1)}, u32[]{:S(2)}, u32[]{:S(2)}) async-start(bf16[2,2,8,64,512]{4,3,1,0,2:T(8,128)(2,1)} %copy.11), calls=%async_computation.1 | async-start | bytes 4194304 | tf_op jit(solution)/shard_map/all_to_all | solution.py:58
  23.1 4.5 %conditional.6 = (bf16[2,2,512,512]{3,2,1,0:T(8,128)(2,1)S(1)}) conditional(s32[]{:T(128)} %bitcast.38, (bf16[2,2,512,512]{3,2,1,0:T(8,128)(2,1)}, bf16[2,2,512,512]{3,2,1,0:T(8,128)(2,1)S(1)}) %tuple.32, (bf16[2,2,512,512]{3,2,1,0:T(8,128)(2,1)S(1)}, bf16[2,2,512,512]{3,2,1,0:T(8,128)(2,1)}) %tuple.33), branch_computations={%region_0.0_spmd, %region_1.0_spmd} | conditional | flops 2150629376 | bytes 31457316
  23.1 2.1 %fusion.18 = f32[2,512,512]{2,1,0:T(8,128)S(1)} fusion(bf16[2,2,512,512]{3,2,1,0:T(8,128)(2,1)} %get-tuple-element.47, bf16[2,2,512,512]{3,2,1,0:T(8,128)(2,1)S(1)} %get-tuple-element.46), kind=kOutput, calls=%fused_computation.24 | convolution fusion | flops 536870912 | bytes 4194304 | tf_op jit(solution)/shard_map/cond/branch_1_fun/bij,bjk->bik/dot_general | solution.py:18
  25.2 0.7 add_bitcast_fusion.1
  25.9 0.7 fusion.24
  26.6 0.7 subtract_bitcast_fusion.1
  27.6 1.5 copy.9
  29.1 39.1 %all-to-all-done.1 = bf16[2,2,8,64,512]{4,3,1,0,2:T(8,128)(2,1)} async-done(((bf16[2,2,8,64,512]{4,3,1,0,2:T(8,128)(2,1)}), bf16[2,2,8,64,512]{4,3,1,0,2:T(8,128)(2,1)}, u32[]{:S(2)}, u32[]{:S(2)}) %all-to-all-start.1) | async-done | bytes 2097184 | tf_op jit(solution)/shard_map/all_to_all | solution.py:58
  68.2 6.5 %all-to-all-start = ((bf16[2,2,8,64,512]{4,3,1,0,2:T(8,128)(2,1)}), bf16[2,2,8,64,512]{4,3,1,0,2:T(8,128)(2,1)}, u32[]{:S(2)}, u32[]{:S(2)}) async-start(bf16[2,2,8,64,512]{4,3,1,0,2:T(8,128)(2,1)} %copy.9), calls=%async_computation | async-start | bytes 4194304 | tf_op jit(solution)/shard_map/all_to_all | solution.py:55
  75.3 1.8 copy.12
  77.1 43.2 %all-to-all-done = bf16[2,2,8,64,512]{4,3,1,0,2:T(8,128)(2,1)} async-done(((bf16[2,2,8,64,512]{4,3,1,0,2:T(8,128)(2,1)}), bf16[2,2,8,64,512]{4,3,1,0,2:T(8,128)(2,1)}, u32[]{:S(2)}, u32[]{:S(2)}) %all-to-all-start) | async-done | bytes 2097184 | tf_op jit(solution)/shard_map/all_to_all | solution.py:55
  120.3 1.8 copy.10
  122.1 3.3 %conditional.8 = (bf16[2,2,512,512]{3,2,1,0:T(8,128)(2,1)S(1)}) conditional(s32[]{:T(128)} %bitcast.37, (bf16[2,2,512,512]{3,2,1,0:T(8,128)(2,1)S(1)}, bf16[2,2,512,512]{3,2,1,0:T(8,128)(2,1)S(1)}) %tuple.55, (bf16[2,2,512,512]{3,2,1,0:T(8,128)(2,1)S(1)}, bf16[2,2,512,512]{3,2,1,0:T(8,128)(2,1)S(1)}) %tuple.56), branch_computations={%region_4.0_spmd, %region_5.0_spmd} | conditional | flops 2150629376 | bytes 23068680
  122.1 0.7 fusion.72
  122.9 0.7 add_bitcast_fusion.4
  123.6 0.7 fusion.78
  124.3 0.7 subtract_bitcast_fusion.4
  125.6 51.6 %all_to_all.45 = bf16[2,2,8,64,512]{4,3,1,0,2:T(8,128)(2,1)S(1)} all-to-all(bf16[2,2,8,64,512]{4,3,1,0,2:T(8,128)(2,1)S(1)} %copy.13), channel_id=1, replica_groups=mesh['cuts'=2,'mode'=8,'branch'=2] {'mode'}, dimensions={2} | all-to-all | bytes 4194304 | tf_op jit(solution)/shard_map/all_to_all | solution.py:66
  177.2 1.5 copy.14
  178.7 2.0 %collective-permute-start = (bf16[2,2,512,512]{3,2,1,0:T(8,128)(2,1)}, bf16[2,2,512,512]{3,2,1,0:T(8,128)(2,1)}, u32[]{:S(2)}, u32[]{:S(2)}) collective-permute-start(bf16[2,2,512,512]{3,2,1,0:T(8,128)(2,1)} %bitcast.59), channel_id=1, source_target_pairs={{0,1},{1,0},{2,3},{3,2},{4,5},{5,4},{6,7},{7,6},{8,9},{9,8},{10,11... | collective-permute-start | bytes 6291464 | tf_op jit(solution)/shard_map/ppermute | solution.py:10
  181.3 1.7 slice_bitcast_fusion.9
  183.3 1.5 collective-permute-done
  184.8 2.6 %broadcast_select_fusion.3 = (bf16[2,2,512,512]{3,2,1,0:T(8,128)(2,1)S(1)}, bf16[2,2,512,512]{3,2,1,0:T(8,128)(2,1)S(1)}, bf16[2,2,512,512]{3,2,1,0:T(8,128)(2,1)S(1)}) fusion(pred[]{:T(512)} %bitcast.36, bf16[2,2,512,512]{3,2,1,0:T(8,128)(2,1)} %collective-permute-done, bf16[2,2,512,512]{3,2,1,0:T(8,128)(2,1)} %bitcast.59, pred[]{:T(512)S(6)} %eq.28), kind=kLoop, calls=%fused_computation.134 | loop fusion | flops 3145728 | bytes 10485762 | tf_op jit(solution)/shard_map/jit(_where)/select_n | solution.py:79
  191.3 1.5 pad_maximum_fusion.6
  (25 shorter events, 5.8 us)
Async XLA Ops:
  0.0 5.7 %copy-start.6 = (s32[7]{0:T(128)S(1)}, s32[7]{0:T(128)}, u32[]{:S(2)}) copy-start(s32[7]{0:T(128)} %param.11) | copy-start | bytes 88
  7.0 2.4 %copy-start.2 = (bf16[2,2,512,512]{3,2,1,0:T(8,128)(2,1)S(1)}, bf16[2,2,512,512]{3,2,1,0:T(8,128)(2,1)}, u32[]{:S(2)}) copy-start(bf16[2,2,512,512]{3,2,1,0:T(8,128)(2,1)} %get-tuple-element.49) | copy-start | bytes 6291460 | tf_op jit(solution)/shard_map/conditional.1
  7.1 2.8 %copy-start.4 = (bf16[2,2,512,512]{3,2,1,0:T(8,128)(2,1)S(1)}, bf16[2,2,512,512]{3,2,1,0:T(8,128)(2,1)}, u32[]{:S(2)}) copy-start(bf16[2,2,512,512]{3,2,1,0:T(8,128)(2,1)} %get-tuple-element.48) | copy-start | bytes 6291460 | tf_op jit(solution)/shard_map/conditional.1
  16.8 51.4 %all-to-all-start.1 = ((bf16[2,2,8,64,512]{4,3,1,0,2:T(8,128)(2,1)}), bf16[2,2,8,64,512]{4,3,1,0,2:T(8,128)(2,1)}, u32[]{:S(2)}, u32[]{:S(2)}) async-start(bf16[2,2,8,64,512]{4,3,1,0,2:T(8,128)(2,1)} %copy.11), calls=%async_computation.1 | async-start | bytes 4194304 | tf_op jit(solution)/shard_map/all_to_all | solution.py:58
  23.1 2.1 %copy-start.1 = (bf16[2,2,512,512]{3,2,1,0:T(8,128)(2,1)S(1)}, bf16[2,2,512,512]{3,2,1,0:T(8,128)(2,1)}, u32[]{:S(2)}) copy-start(bf16[2,2,512,512]{3,2,1,0:T(8,128)(2,1)} %get-tuple-element.47) | copy-start | bytes 6291460 | tf_op jit(solution)/shard_map/conditional
  68.2 52.2 %all-to-all-start = ((bf16[2,2,8,64,512]{4,3,1,0,2:T(8,128)(2,1)}), bf16[2,2,8,64,512]{4,3,1,0,2:T(8,128)(2,1)}, u32[]{:S(2)}, u32[]{:S(2)}) async-start(bf16[2,2,8,64,512]{4,3,1,0,2:T(8,128)(2,1)} %copy.9), calls=%async_computation | async-start | bytes 4194304 | tf_op jit(solution)/shard_map/all_to_all | solution.py:55
  177.2 4.1 %copy-start.7 = (s32[2]{0:T(128)S(1)}, s32[2]{0:T(128)}, u32[]{:S(2)}) copy-start(s32[2]{0:T(128)} %param.12) | copy-start | bytes 28
  178.7 6.1 %collective-permute-start = (bf16[2,2,512,512]{3,2,1,0:T(8,128)(2,1)}, bf16[2,2,512,512]{3,2,1,0:T(8,128)(2,1)}, u32[]{:S(2)}, u32[]{:S(2)}) collective-permute-start(bf16[2,2,512,512]{3,2,1,0:T(8,128)(2,1)} %bitcast.59), channel_id=1, source_target_pairs={{0,1},{1,0},{2,3},{3,2},{4,5},{5,4},{6,7},{7,6},{8,9},{9,8},{10,11... | collective-permute-start | bytes 6291464 | tf_op jit(solution)/shard_map/ppermute | solution.py:10
where the time goes:
time: 196 us; the launch traced here: 193 us
  waiting for transfers between devices  83.8 us (43%)
  blocking collectives  51.6 us (26%)
  local copies, waits for them, and re-layouts  18.6 us (9%)
  matrix products  15.1 us (8%)
  starting transfers between devices  14.1 us (7%)
  other arithmetic  6.63 us (3%)
  between operations  2.74 us (1%)
    all_to_all x1, blocking collectives, per_device(): lax.all_to_all(split_rows(middle, blocks), 'mode', split_axis=2, concat_a...  51.6 us
    all_to_all x1, waiting for transfers between devices, per_device(): lax.all_to_all(split_rows(first_pair, blocks), 'mode', split_axis=2, conc...  43.2 us
    all_to_all x1, waiting for transfers between devices, per_device(): lax.all_to_all(split_rows(second_pair, blocks), 'mode', split_axis=2, con...  39.1 us
    all_to_all x1, starting transfers between devices, per_device(): lax.all_to_all(split_rows(first_pair, blocks), 'mode', split_axis=2, conc...  6.45 us
    dot_general x5, matrix products, complex_sums(): jnp.einsum(spec, left_op[0], right_op[1], preferred_element_type=jnp.floa...  6.06 us
    squeeze x1, local copies, waits for them, and re-layouts, per_device(): second_pair = join_pair(leaves[2], leaves[3], join_order[base_index + 1])  5.73 us
    all_to_all x1, starting transfers between devices, per_device(): lax.all_to_all(split_rows(second_pair, blocks), 'mode', split_axis=2, con...  5.66 us
    reshape x3, local copies, waits for them, and re-layouts, split_rows(): tensor.reshape(shape[0], shape[1], blocks, shape[2] // blocks, shape[3])  4.91 us
  transfers between devices with their start and end apart: 3, of which 3 were waited for; matrix products, arithmetic and copies ran while one was open for 5% of the time, Pallas kernels for 0%

commit v1 on v0

v1 whole, which is shorter than its diff:
```python
import functools

import jax
import jax.numpy as jnp
from jax import lax
from jax.experimental import pallas as pl
from jax.experimental.pallas import tpu as pltpu
from jax.sharding import PartitionSpec as P

MESH = pl.DeviceIdType.MESH


def dot(left, right):
    return jnp.dot(left, right, preferred_element_type=jnp.float32)


def complex_rows(left_real, left_imag, right_real, right_imag):
    real_part = dot(left_real, right_real) - dot(left_imag, right_imag)
    imag_part = dot(left_real, right_imag) + dot(left_imag, right_real)
    return real_part, imag_part


def join_kernel(tile, order_ref, left_ref, right_ref, out_ref):
    rows = left_ref.shape[-2]

    @pl.loop(0, rows // tile)
    def _(step):
        at = pl.ds(pl.multiple_of(step * tile, tile), tile)
        real_part, imag_part = complex_rows(
            left_ref[0, 0, 0, at, :],
            left_ref[0, 1, 0, at, :],
            right_ref[0, 0, 0],
            right_ref[0, 1, 0],
        )
        out_ref[0, 0, 0, at, :] = real_part.astype(out_ref.dtype)
        out_ref[0, 1, 0, at, :] = imag_part.astype(out_ref.dtype)


def first_joins(leaves, order):
    _, _, per, m, width = leaves.shape
    block = (1, 2, 1, m, width)
    return pl.pallas_call(
        functools.partial(join_kernel, min(256, m)),
        out_shape=jax.ShapeDtypeStruct((2, 2, per, m, width), leaves.dtype),
        grid_spec=pltpu.PrefetchScalarGridSpec(
            num_scalar_prefetch=1,
            grid=(2, per),
            in_specs=[
                pl.BlockSpec(block, lambda k, e, order: (order[2 * k], 0, e, 0, 0)),
                pl.BlockSpec(block, lambda k, e, order: (order[2 * k + 1], 0, e, 0, 0)),
            ],
            out_specs=pl.BlockSpec(block, lambda k, e, order: (k, 0, e, 0, 0)),
        ),
        name="first_joins",
    )(order, leaves, leaves)


def middle_kernel(
    n, per, prod_ref, out_ref, gathered, result,
    send1, recv1, local1, send3, recv3, local3, sendf, recvf,
):
    group = n // per
    m = lax.axis_index("mode")
    core = lax.axis_index("branch")
    h, g = m // group, m % group
    blk, width = prod_ref.shape[-2:]

    def regroup_copy(t, slot, k):
        to = lax.rem(g + k, group)
        return pltpu.make_async_remote_copy(
            src_ref=prod_ref.at[slot, :, :, per * to + t],
            dst_ref=gathered.at[t, slot, :, pl.ds(per * g, per)],
            send_sem=send1.at[t, slot, k],
            recv_sem=recv1.at[t, slot, k],
            device_id={"mode": h * group + to},
            device_id_type=MESH,
        )

    def regroup_arrival(t, slot, k):
        source = lax.rem(g + group - k, group)
        return pltpu.make_async_remote_copy(
            src_ref=prod_ref.at[slot, :, :, per * g + t],
            dst_ref=gathered.at[t, slot, :, pl.ds(per * source, per)],
            send_sem=send1.at[t, slot, k],
            recv_sem=recv1.at[t, slot, k],
            device_id={"mode": h * group + source},
            device_id_type=MESH,
        )

    def own_copy(t, slot):
        return pltpu.make_async_copy(
            prod_ref.at[slot, :, :, per * g + t],
            gathered.at[t, slot, :, pl.ds(per * g, per)],
            local1.at[t, slot],
        )

    def place(source, t):
        batch = per * (per * lax.rem(source, group) + t) + source // group
        return batch // n, lax.rem(batch, n)

    def deliver_copy(t, k):
        to = lax.rem(m + k, n)
        entry, row = place(m, t)
        return pltpu.make_async_remote_copy(
            src_ref=result.at[t, :, to],
            dst_ref=out_ref.at[core, entry, :, row],
            send_sem=send3.at[t, k],
            recv_sem=recv3.at[t, k],
            device_id={"mode": to},
            device_id_type=MESH,
        )

    def deliver_arrival(t, k):
        source = lax.rem(m + n - k, n)
        entry, row = place(source, t)
        return pltpu.make_async_remote_copy(
            src_ref=result.at[t, :, source],
            dst_ref=out_ref.at[core, entry, :, row],
            send_sem=send3.at[t, k],
            recv_sem=recv3.at[t, k],
            device_id={"mode": source},
            device_id_type=MESH,
        )

    def own_deliver(t):
        entry, row = place(m, t)
        return pltpu.make_async_copy(
            result.at[t, :, m], out_ref.at[core, entry, :, row], local3.at[t]
        )

    def forward_copy(t, k, owner):
        source = lax.rem(m + n - k, n)
        entry, row = place(source, t)
        part = out_ref.at[owner, entry, :, row]
        return pltpu.make_async_remote_copy(
            src_ref=part,
            dst_ref=part,
            send_sem=sendf.at[t, k],
            recv_sem=recvf.at[t, k],
            device_id={"branch": 1 - core},
            device_id_type=MESH,
        )

    barrier = pltpu.get_barrier_semaphore()
    for k in range(1, n):
        pl.semaphore_signal(
            barrier, inc=1, device_id={"mode": lax.rem(m + k, n)}, device_id_type=MESH
        )
    pl.semaphore_signal(barrier, inc=1, device_id={"branch": 1 - core}, device_id_type=MESH)
    pl.semaphore_wait(barrier, n)

    for t in range(per):
        for slot in range(2):
            for k in range(1, group):
                regroup_copy(t, slot, k).start()
            own_copy(t, slot).start()

    tile_blocks = max(1, min(n, 256 // blk))
    tile = tile_blocks * blk
    for t in range(per):
        for slot in range(2):
            own_copy(t, slot).wait()
            for k in range(1, group):
                regroup_arrival(t, slot, k).wait_recv()

        @pl.loop(0, n // tile_blocks)
        def _(step):
            at = pl.ds(step * tile_blocks, tile_blocks)
            real_part, imag_part = complex_rows(
                gathered[t, 1, 0, at].reshape(tile, width),
                gathered[t, 1, 1, at].reshape(tile, width),
                gathered[t, 0, 0].reshape(n * blk, width),
                gathered[t, 0, 1].reshape(n * blk, width),
            )
            shape = (tile_blocks, blk, width)
            result[t, 0, at] = real_part.astype(result.dtype).reshape(shape)
            result[t, 1, at] = imag_part.astype(result.dtype).reshape(shape)

        for k in range(1, n):
            deliver_copy(t, k).start()
        own_deliver(t).start()

    for t in range(per):
        own_deliver(t).wait()
        forward_copy(t, 0, core).start()
        for k in range(1, n):
            deliver_arrival(t, k).wait_recv()
            forward_copy(t, k, core).start()

    for t in range(per):
        for slot in range(2):
            for k in range(1, group):
                regroup_copy(t, slot, k).wait_send()
        for k in range(1, n):
            deliver_copy(t, k).wait_send()
        for k in range(n):
            forward_copy(t, k, core).wait_send()
            forward_copy(t, k, 1 - core).wait_recv()


def middle_join(products, n, per):
    _, _, _, _, blk, width = products.shape
    group = n // per
    dma = pltpu.SemaphoreType.DMA
    return pl.pallas_call(
        functools.partial(middle_kernel, n, per),
        out_shape=jax.ShapeDtypeStruct((2, per, 2, n, blk, width), products.dtype),
        in_specs=[pl.BlockSpec(memory_space=pl.ANY)],
        out_specs=pl.BlockSpec(memory_space=pl.ANY),
        scratch_shapes=[
            pltpu.VMEM((per, 2, 2, n, blk, width), products.dtype),
            pltpu.VMEM((per, 2, n, blk, width), products.dtype),
            dma((per, 2, group)),
            dma((per, 2, group)),
            dma((per, 2)),
            dma((per, n)),
            dma((per, n)),
            dma((per,)),
            dma((per, n)),
            dma((per, n)),
        ],
        compiler_params=pltpu.CompilerParams(collective_id=0, has_side_effects=True),
        name="middle_join",
    )(products)


def top_kernel(picks_ref, left_ref, right_ref, chosen_ref, out_ref):
    top_real, top_imag = complex_rows(
        left_ref[0, 0, 0], left_ref[0, 0, 1], right_ref[0, 0, 0], right_ref[0, 0, 1]
    )
    dtype = left_ref.dtype
    real_part, imag_part = complex_rows(
        top_real.astype(dtype), top_imag.astype(dtype), chosen_ref[0, 0], chosen_ref[0, 1]
    )
    out_ref[0, 0] = real_part
    out_ref[1, 0] = imag_part


def top_join(middles, boundary, picks, per):
    m, width = boundary.shape[-2:]
    half = m // 2
    return pl.pallas_call(
        top_kernel,
        out_shape=jax.ShapeDtypeStruct((2, per, half, width), jnp.float32),
        grid_spec=pltpu.PrefetchScalarGridSpec(
            num_scalar_prefetch=1,
            grid=(per,),
            in_specs=[
                pl.BlockSpec((1, 1, 2, half, width), lambda e, p: (p[0], e, 0, p[1], 0)),
                pl.BlockSpec((1, 1, 2, m, width), lambda e, p: (1 - p[0], e, 0, 0, 0)),
                pl.BlockSpec((1, 2, m, width), lambda e, p: (p[2 + e], 0, 0, 0)),
            ],
            out_specs=pl.BlockSpec((2, 1, half, width), lambda e, p: (0, e, 0, 0)),
        ),
        name="top_join",
    )(picks, middles, middles, boundary)


def per_device(leaves, join_order, slice_values, boundary):
    n = lax.axis_size("mode")
    core = lax.axis_index("branch")
    _, _, per, m, width = leaves.shape
    order = join_order.astype(jnp.int32)
    own = lax.dynamic_slice_in_dim(order, 2 * core, 2)
    middle_order = lax.dynamic_slice_in_dim(order, 4 + core, 1)[0]
    right_pair = 1 - middle_order
    left_pair = middle_order
    right_flag = jnp.where(right_pair == 1, own[1], own[0])
    left_flag = jnp.where(left_pair == 1, own[1], own[0])
    leaf_order = jnp.stack(
        [
            2 * right_pair + right_flag,
            2 * right_pair + 1 - right_flag,
            2 * left_pair + left_flag,
            2 * left_pair + 1 - left_flag,
        ]
    )
    products = first_joins(leaves, leaf_order)
    products = products.reshape(2, 2, per, n, m // n, width)
    middles = middle_join(products, n, per).reshape(2, per, 2, m, width)
    picks = jnp.concatenate([order[6:7], core[None].astype(jnp.int32), slice_values])
    return top_join(middles, boundary, picks, per)


def solution(mesh):
    in_specs = (P("branch", None, ("cuts", "mode"), None, None), P(), P(("cuts", "mode")), P())
    out_specs = P(None, ("cuts", "mode"), "branch", None)
    return jax.shard_map(
        per_device, mesh=mesh, in_specs=in_specs, out_specs=out_specs, check_vma=False
    )
```

time: 196 us -> 119 us (0.61)
  the two profiles are of different devices: /device:TPU:13 before, /device:TPU:29 now
where the time goes in v1:
time: 119 us; the launch traced here: 118 us
  Pallas kernels  108 us (91%)
  between operations  4.44 us (4%)
  local copies, waits for them, and re-layouts  2.7 us (2%)
  other arithmetic  2.55 us (2%)
    pallas_call x1, Pallas kernels, middle_join(): pl.pallas_call(functools.partial(middle_kernel, n, per), out_shape=jax.Sh...  93 us
    pallas_call x1, Pallas kernels, first_joins(): pl.pallas_call(functools.partial(join_kernel, min(256, m)), out_shape=jax...  9.57 us
    pallas_call x1, Pallas kernels, top_join(): pl.pallas_call(top_kernel, out_shape=jax.ShapeDtypeStruct((2, per, half,...  5.92 us

profile of v1, /device:TPU:29, one launch (start us, length us, event | category | flops | bytes accessed | tf_op | source)
XLA Modules:
  0.0 118.2 jit_solution(9918863658707241958)
XLA Ops:
  0.0 0.7 dynamic_slice.7
  0.7 0.6 fusion
  1.3 1.4 %fusion.1 = (s32[1]{0:T(128)}, s32[1]{0:T(128)}) fusion(s32[7]{0:T(128)} %param.5, s32[]{:T(128)S(6)} %select_n.19), kind=kLoop, calls=%fused_computation.3 | loop fusion | bytes 20 | tf_op jit(solution)/shard_map/dynamic_slice | solution.py:265
  7.1 0.7 pad_add_fusion.1.order_ref
  7.8 1.9 %pad_add_fusion.picks_ref = s32[4]{0:T(128)} fusion(s32[2]{0:T(128)} %param.6, s32[1]{0:T(128)} %bitcast, s32[1]{0:T(128)} %get-tuple-element.8), kind=kLoop, calls=%fused_computation | loop fusion | flops 8 | bytes 32 | tf_op jit(solution)/shard_map/concatenate | solution.py:281
  9.7 9.6 %first_joins.1 = bf16[2,2,2,512,512]{4,3,2,1,0:T(8,128)(2,1)} custom-call(s32[4]{0:T(128)} %pad_add_fusion.1.order_ref, bf16[4,2,2,512,512]{4,3,2,1,0:T(8,128)(2,1)} %right_ref.1, bf16[4,2,2,512,512]{4,3,2,1,0:T(8,128)(2,1)} %right_ref.1), custom_call_target="tpu_custom_call" | custom-call | tf_op jit(solution)/shard_map/first_joins/pallas_call | solution.py:42
  19.2 93.0 %middle_join.1 = bf16[2,2,2,8,64,512]{5,4,3,2,1,0:T(8,128)(2,1)} custom-call(bf16[2,2,2,8,64,512]{5,4,3,2,1,0:T(8,128)(2,1)} %bitcast.13), custom_call_target="tpu_custom_call" | custom-call | tf_op jit(solution)/shard_map/middle_join/pallas_call | solution.py:205
  112.3 5.9 %top_join.1 = f32[2,2,256,512]{3,2,1,0:T(8,128)} custom-call(s32[4]{0:T(128)} %pad_add_fusion.picks_ref, bf16[2,2,2,512,512]{4,3,2,1,0:T(8,128)(2,1)} %bitcast.11, bf16[2,2,2,512,512]{4,3,2,1,0:T(8,128)(2,1)} %bitcast.12, bf16[2,2,512,512]{3,2,1,0:T(8,128)(2,1)} %chosen_ref.1), custom_call_target="tpu_custom_call" | custom-call | tf_op jit(solution)/shard_map/top_join/pallas_call | solution.py:242

commit v2 on v0

v2 whole, which is shorter than its diff:
```python
import functools

import jax
import jax.numpy as jnp
from jax import lax
from jax.experimental import pallas as pl
from jax.experimental.pallas import tpu as pltpu
from jax.sharding import PartitionSpec as P

MESH = pl.DeviceIdType.MESH


def dot(left, right):
    return jnp.dot(left, right, preferred_element_type=jnp.float32)


def complex_rows(left_real, left_imag, right_real, right_imag):
    real_part = dot(left_real, right_real) - dot(left_imag, right_imag)
    imag_part = dot(left_real, right_imag) + dot(left_imag, right_real)
    return real_part, imag_part


def contract_kernel(
    per, order_ref, leaves_ref, out_ref, prod, right, left, result,
    leaf_sem, own_right, own_left,
    cross_right_send, cross_right_recv, cross_left_send, cross_left_recv,
    column_send, column_recv, relay_send, relay_recv,
    deliver_send, deliver_recv, forward_send, forward_recv, *leaf,
):
    n = lax.axis_size("mode")
    group = n // per
    pair = 2
    peers = group // pair
    rounds = n // pair
    wide = pair * per
    m = lax.axis_index("mode")
    core = lax.axis_index("branch")
    h, g = m // group, lax.rem(m, group)
    line, side = g // pair, lax.rem(g, pair)
    across = pair * line + 1 - side
    blk, width = out_ref.shape[-2:]
    order = n * blk

    def remote(src, dst, send, recv, **device):
        return pltpu.make_async_remote_copy(
            src_ref=src,
            dst_ref=dst,
            send_sem=send,
            recv_sem=recv,
            device_id=device,
            device_id_type=MESH,
        )

    def column(line_at):
        return pair * line_at + side

    def up(k):
        return lax.rem(line + k, peers)

    def down(k):
        return lax.rem(line + peers - k, peers)

    def own_right_copy(q, e):
        return pltpu.make_async_copy(
            prod.at[0, :, e, pair * q + side], right.at[q, :, per * g + e], own_right.at[q, e]
        )

    def own_left_copy(q, e):
        return pltpu.make_async_copy(
            prod.at[1, :, e, pair * q + side], left.at[q, :, per * side + e], own_left.at[q, e]
        )

    def cross_right(q, e, source=None):
        return remote(
            prod.at[0, :, e, pair * q + 1 - side],
            right.at[q, :, per * (g if source is None else source) + e],
            cross_right_send.at[q, e],
            cross_right_recv.at[q, e],
            mode=h * group + across,
        )

    def cross_left(q, e, source=None):
        return remote(
            prod.at[1, :, e, pair * q + 1 - side],
            left.at[q, :, per * (side if source is None else source) + e],
            cross_left_send.at[q, e],
            cross_left_recv.at[q, e],
            mode=h * group + across,
        )

    def column_right(q, e, k, target, source):
        return remote(
            prod.at[0, :, e, pair * q + side],
            right.at[q, :, per * column(source) + e],
            column_send.at[q, e, k],
            column_recv.at[q, e, k],
            mode=h * group + column(target),
        )

    def relay_right(q, e, k, target, source):
        part = right.at[q, :, per * (pair * source + 1 - side) + e]
        return remote(
            part,
            part,
            relay_send.at[q, e, k],
            relay_recv.at[q, e, k],
            mode=h * group + column(target),
        )

    def spot(q, h_from, side_from):
        batch = per * (pair * q + side_from) + h_from
        return batch // n, lax.rem(batch, n)

    def deliver(q, i):
        entry, row = spot(q, h, side)
        at = pair * h + side
        return remote(
            result.at[q, :, i],
            out_ref.at[core, entry, :, row],
            deliver_send.at[q, i],
            deliver_recv.at[q, at],
            mode=wide * line + i,
        )

    def deliver_own(q, i):
        entry, row = spot(q, h, side)
        return pltpu.make_async_copy(
            result.at[q, :, i],
            out_ref.at[core, entry, :, row],
            deliver_recv.at[q, pair * h + side],
        )

    def delivered(q, h_from, side_from):
        entry, row = spot(q, h_from, side_from)
        part = out_ref.at[core, entry, :, row]
        return pltpu.make_async_copy(part, part, deliver_recv.at[q, pair * h_from + side_from])

    def forward(q, h_from, side_from, owner):
        entry, row = spot(q, h_from, side_from)
        part = out_ref.at[owner, entry, :, row]
        at = pair * h_from + side_from
        return remote(
            part, part, forward_send.at[q, at], forward_recv.at[q, at], branch=1 - core
        )

    def leaf_copy(e):
        return pltpu.make_async_copy(leaves_ref.at[:, :, e], leaf[e], leaf_sem.at[e])

    middle_order = order_ref[4 + core]
    tile = min(256, order)

    def first_join(slot, e):
        which = 1 - middle_order if slot == 0 else middle_order
        flag = order_ref[2 * core + which]
        left_leaf = 2 * which + flag
        right_leaf = 2 * which + 1 - flag

        @pl.loop(0, order // tile)
        def _(step):
            at = pl.ds(pl.multiple_of(step * tile, tile), tile)
            real_part, imag_part = complex_rows(
                leaf[e][left_leaf, 0, at, :],
                leaf[e][left_leaf, 1, at, :],
                leaf[e][right_leaf, 0],
                leaf[e][right_leaf, 1],
            )
            blocks = tile // blk
            shape = (blocks, blk, width)
            to = pl.ds(step * blocks, blocks)
            prod[slot, 0, e, to] = real_part.astype(prod.dtype).reshape(shape)
            prod[slot, 1, e, to] = imag_part.astype(prod.dtype).reshape(shape)

    def send_cross_right(q, e):
        cross_right(q, e).start()

    def send_column(q, e):
        for k in range(1, peers):
            column_right(q, e, k, up(k), line).start()
        own_right_copy(q, e).start()

    def send_cross_left(q, e):
        cross_left(q, e).start()
        own_left_copy(q, e).start()

    def send_relay(q, e):
        cross_right(q, e, across).wait_recv()
        for k in range(1, peers):
            relay_right(q, e, k, up(k), line).start()

    barrier = pltpu.get_barrier_semaphore()
    for k in range(1, n):
        pl.semaphore_signal(
            barrier, inc=1, device_id={"mode": lax.rem(m + k, n)}, device_id_type=MESH
        )
    pl.semaphore_signal(barrier, inc=1, device_id={"branch": 1 - core}, device_id_type=MESH)
    for e in range(per):
        leaf_copy(e).start()

    for e in range(per):
        leaf_copy(e).wait()
        first_join(0, e)
        if e == 0:
            pl.semaphore_wait(barrier, n)
        send_cross_right(0, e)
        send_column(0, e)
    for e in range(per):
        first_join(1, e)
        send_cross_left(0, e)
        send_relay(0, e)
    for q in range(1, rounds):
        for e in range(per):
            send_cross_right(q, e)
        for e in range(per):
            send_cross_left(q, e)

    row_tile = wide * blk
    for q in range(rounds):
        if q + 1 < rounds:
            for e in range(per):
                send_column(q + 1, e)
        for e in range(per):
            own_right_copy(q, e).wait()
            own_left_copy(q, e).wait()
            cross_left(q, e, 1 - side).wait_recv()
            for k in range(1, peers):
                column_right(q, e, k, down(k), down(k)).wait_recv()
                relay_right(q, e, k, down(k), down(k)).wait_recv()

        real_part, imag_part = complex_rows(
            left[q, 0].reshape(row_tile, width),
            left[q, 1].reshape(row_tile, width),
            right[q, 0].reshape(order, width),
            right[q, 1].reshape(order, width),
        )
        result[q, 0] = real_part.astype(result.dtype).reshape(wide, blk, width)
        result[q, 1] = imag_part.astype(result.dtype).reshape(wide, blk, width)

        for i in range(wide):
            here = wide * line + i == m

            @pl.when(jnp.logical_not(here))
            def _():
                deliver(q, i).start()

            @pl.when(here)
            def _():
                deliver_own(q, i).start()

        if q + 1 < rounds:
            for e in range(per):
                send_relay(q + 1, e)

    for q in range(rounds):
        for h_from in range(per):
            for side_from in range(pair):
                delivered(q, h_from, side_from).wait()
                forward(q, h_from, side_from, core).start()

    for q in range(rounds):
        for e in range(per):
            cross_right(q, e).wait_send()
            cross_left(q, e).wait_send()
            for k in range(1, peers):
                column_right(q, e, k, up(k), line).wait_send()
                relay_right(q, e, k, up(k), line).wait_send()
        for i in range(wide):

            @pl.when(wide * line + i != m)
            def _():
                deliver(q, i).wait_send()

        for h_from in range(per):
            for side_from in range(pair):
                forward(q, h_from, side_from, core).wait_send()
                forward(q, h_from, side_from, 1 - core).wait_recv()


def lower_levels(leaves, join_order):
    n = lax.axis_size("mode")
    count, _, per, order, width = leaves.shape
    blk = order // n
    rounds, peers, wide = n // 2, n // per // 2, 2 * per
    dma = pltpu.SemaphoreType.DMA
    dtype = leaves.dtype
    return pl.pallas_call(
        functools.partial(contract_kernel, per),
        out_shape=jax.ShapeDtypeStruct((2, per, 2, n, blk, width), dtype),
        in_specs=[
            pl.BlockSpec(memory_space=pltpu.SMEM),
            pl.BlockSpec(memory_space=pl.ANY),
        ],
        out_specs=pl.BlockSpec(memory_space=pl.ANY),
        scratch_shapes=[
            pltpu.VMEM((2, 2, per, n, blk, width), dtype),
            pltpu.VMEM((rounds, 2, n, blk, width), dtype),
            pltpu.VMEM((rounds, 2, wide, blk, width), dtype),
            pltpu.VMEM((rounds, 2, wide, blk, width), dtype),
            dma((per,)),
            dma((rounds, per)),
            dma((rounds, per)),
            dma((rounds, per)),
            dma((rounds, per)),
            dma((rounds, per)),
            dma((rounds, per)),
            dma((rounds, per, peers)),
            dma((rounds, per, peers)),
            dma((rounds, per, peers)),
            dma((rounds, per, peers)),
            dma((rounds, wide)),
            dma((rounds, wide)),
            dma((rounds, wide)),
            dma((rounds, wide)),
        ]
        + [pltpu.VMEM((count, 2, order, width), dtype)] * per,
        compiler_params=pltpu.CompilerParams(collective_id=0, has_side_effects=True),
        name="lower_levels",
    )(join_order, leaves)


def top_kernel(order_ref, slices_ref, left_ref, right_ref, chosen_ref, out_ref):
    half = out_ref.shape[-2]
    at = pl.ds(pl.multiple_of(lax.axis_index("branch") * half, half), half)
    top_real, top_imag = complex_rows(
        left_ref[0, 0, 0, at, :], left_ref[0, 0, 1, at, :], right_ref[0, 0, 0], right_ref[0, 0, 1]
    )
    dtype = left_ref.dtype
    real_part, imag_part = complex_rows(
        top_real.astype(dtype), top_imag.astype(dtype), chosen_ref[0, 0], chosen_ref[0, 1]
    )
    out_ref[0, 0] = real_part
    out_ref[1, 0] = imag_part


def top_join(middles, boundary, join_order, slice_values, per):
    order, width = boundary.shape[-2:]
    half = order // 2
    last = join_order.shape[0] - 1
    return pl.pallas_call(
        top_kernel,
        out_shape=jax.ShapeDtypeStruct((2, per, half, width), jnp.float32),
        grid_spec=pltpu.PrefetchScalarGridSpec(
            num_scalar_prefetch=2,
            grid=(per,),
            in_specs=[
                pl.BlockSpec((1, 1, 2, order, width), lambda e, o, s: (o[last], e, 0, 0, 0)),
                pl.BlockSpec((1, 1, 2, order, width), lambda e, o, s: (1 - o[last], e, 0, 0, 0)),
                pl.BlockSpec((1, 2, order, width), lambda e, o, s: (s[e], 0, 0, 0)),
            ],
            out_specs=pl.BlockSpec((2, 1, half, width), lambda e, o, s: (0, e, 0, 0)),
        ),
        name="top_join",
    )(join_order, slice_values, middles, middles, boundary)


def per_device(leaves, join_order, slice_values, boundary):
    _, _, per, order, width = leaves.shape
    middles = lower_levels(leaves, join_order).reshape(2, per, 2, order, width)
    return top_join(middles, boundary, join_order, slice_values, per)


def solution(mesh):
    in_specs = (P("branch", None, ("cuts", "mode"), None, None), P(), P(("cuts", "mode")), P())
    out_specs = P(None, ("cuts", "mode"), "branch", None)
    return jax.shard_map(
        per_device, mesh=mesh, in_specs=in_specs, out_specs=out_specs, check_vma=False
    )
```

time: 196 us -> 92 us (0.47); the launches traced: 193 us -> 91.8 us
  Pallas kernels: 0 us -> 91.8 us
  waiting for transfers between devices: 83.8 us -> 0 us
  blocking collectives: 51.6 us -> 0 us
  local copies, waits for them, and re-layouts: 18.6 us -> 0 us
  matrix products: 15.1 us -> 0 us
  starting transfers between devices: 14.1 us -> 0 us
  other arithmetic: 6.63 us -> 0 us
  between operations: 2.74 us -> 0.01 us
    pallas_call x0 -> x2, Pallas kernels: none -> 91.8 us  [the longest x1 85.7 us: lower_levels(): pl.pallas_call(functools.partial(contract_kernel, per), out_shape=jax.Sha...]
    all_to_all x2 -> x0, waiting for transfers between devices: 82.3 us -> none  [the longest x1 43.2 us: per_device(): lax.all_to_all(split_rows(first_pair, blocks), 'mode', split_axis=2, conc...]
    all_to_all x1 -> x0, blocking collectives: 51.6 us -> none  [per_device(): lax.all_to_all(split_rows(middle, blocks), 'mode', split_axis=2, concat_a...]
    dot_general x20 -> x0, matrix products: 15.1 us -> none  [the longest x5 6.06 us: complex_sums(): jnp.einsum(spec, left_op[0], right_op[1], preferred_element_type=jnp.floa...]
    all_to_all x2 -> x0, starting transfers between devices: 12.1 us -> none  [the longest x1 6.45 us: per_device(): lax.all_to_all(split_rows(first_pair, blocks), 'mode', split_axis=2, conc...]
    squeeze x1 -> x0, local copies, waits for them, and re-layouts: 5.73 us -> none  [per_device(): second_pair = join_pair(leaves[2], leaves[3], join_order[base_index + 1])]
    all_to_all x3 -> x0, local copies, waits for them, and re-layouts: 5.14 us -> none  [the longest x1 1.81 us: per_device(): lax.all_to_all(split_rows(first_pair, blocks), 'mode', split_axis=2, conc...]
    reshape x3 -> x0, local copies, waits for them, and re-layouts: 4.91 us -> none  [split_rows(): tensor.reshape(shape[0], shape[1], blocks, shape[2] // blocks, shape[3])]
  transfers between devices with their start and end apart: 3 -> 0, of which waited for: 3 -> 0; matrix products, arithmetic and copies ran while one was open for 5% -> 0% of each run, Pallas kernels for 0% -> 0%
where the time goes in v2:
time: 92 us; the launch traced here: 91.8 us
  Pallas kernels  91.8 us (100%)
    pallas_call x1, Pallas kernels, lower_levels(): pl.pallas_call(functools.partial(contract_kernel, per), out_shape=jax.Sha...  85.7 us
    pallas_call x1, Pallas kernels, top_join(): pl.pallas_call(top_kernel, out_shape=jax.ShapeDtypeStruct((2, per, half,...  6.08 us

profile of v2, /device:TPU:13, one launch (start us, length us, event | category | flops | bytes accessed | tf_op | source)
XLA Modules:
  0.0 91.8 jit_solution(9436951426521113589)
XLA Ops:
  0.0 85.7 %lower_levels.1 = bf16[2,2,2,8,64,512]{5,4,3,2,1,0:T(8,128)(2,1)} custom-call(s32[7]{0:T(128)} %order_ref.3, bf16[4,2,2,512,512]{4,3,2,1,0:T(8,128)(2,1)} %leaves_ref.1), custom_call_target="tpu_custom_call" | custom-call | tf_op jit(solution)/shard_map/lower_levels/pallas_call | solution.py:285
  85.7 6.1 %top_join.1 = f32[2,2,256,512]{3,2,1,0:T(8,128)} custom-call(s32[7]{0:T(128)} %order_ref.3, s32[2]{0:T(128)} %slices_ref.1, bf16[2,2,2,512,512]{4,3,2,1,0:T(8,128)(2,1)} %bitcast.1, bf16[2,2,2,512,512]{4,3,2,1,0:T(8,128)(2,1)} %bitcast.2, bf16[2,2,512,512]{3,2,1,0:T(8,128)(2,1)} %chosen_ref.1), custom_call_target="tpu_custom_call" | custom-call | tf_op jit(solution)/shard_map/top_join/pallas_call | solution.py:338

commit v3 on v2

--- a/solution.py
+++ b/solution.py
@@ -203,21 +203,54 @@
             pl.semaphore_wait(barrier, n)
         send_cross_right(0, e)
         send_column(0, e)
+    ahead = min(2, rounds)
+    for q in range(1, ahead):
+        for e in range(per):
+            send_cross_right(q, e)
+            send_column(q, e)
     for e in range(per):
         first_join(1, e)
         send_cross_left(0, e)
-        send_relay(0, e)
-    for q in range(1, rounds):
+    for q in range(ahead, rounds):
         for e in range(per):
             send_cross_right(q, e)
         for e in range(per):
+            send_cross_left(q - 1, e)
+    for q in range(max(1, rounds - 1), rounds):
+        for e in range(per):
             send_cross_left(q, e)
+    for q in range(ahead):
+        for e in range(per):
+            send_relay(q, e)
+    for q in range(ahead, min(ahead + 1, rounds)):
+        for e in range(per):
+            send_column(q, e)
+
+    def send_results(q, late):
+        for i in range(wide):
+            target = wide * line + i
+            same_group = target // group == h
+            same_line = lax.rem(target, group) // pair == line
+            waits = jnp.logical_and(same_group, jnp.logical_not(same_line))
+            if late:
+
+                @pl.when(waits)
+                def _():
+                    deliver(q, i).start()
+
+            else:
+
+                @pl.when(jnp.logical_not(jnp.logical_or(waits, target == m)))
+                def _():
+                    deliver(q, i).start()
+
+                @pl.when(target == m)
+                def _():
+                    deliver_own(q, i).start()
 
     row_tile = wide * blk
+    held = []
     for q in range(rounds):
-        if q + 1 < rounds:
-            for e in range(per):
-                send_column(q + 1, e)
         for e in range(per):
             own_right_copy(q, e).wait()
             own_left_copy(q, e).wait()
@@ -235,20 +268,18 @@
         result[q, 0] = real_part.astype(result.dtype).reshape(wide, blk, width)
         result[q, 1] = imag_part.astype(result.dtype).reshape(wide, blk, width)
 
-        for i in range(wide):
-            here = wide * line + i == m
-
-            @pl.when(jnp.logical_not(here))
-            def _():
-                deliver(q, i).start()
-
-            @pl.when(here)
-            def _():
-                deliver_own(q, i).start()
-
-        if q + 1 < rounds:
+        send_results(q, False)
+        held.append(q)
+        for later in range(q + ahead, min(q + ahead + 1, rounds)):
             for e in range(per):
-                send_relay(q + 1, e)
+                send_relay(later, e)
+        for later in range(q + ahead + 1, min(q + ahead + 2, rounds)):
+            for e in range(per):
+                send_column(later, e)
+        if q + ahead + 1 >= rounds:
+            for earlier in held:
+                send_results(earlier, True)
+            held = []
 
     for q in range(rounds):
         for h_from in range(per):

time: 92 us -> 94.8 us (1.030)
  Pallas kernels: 91.8 us -> 94.6 us
    pallas_call x1, Pallas kernels: 85.7 us -> 88.5 us  [lower_levels(): pl.pallas_call(functools.partial(contract_kernel, per), out_shape=jax.Sha...]
where the time goes in v3:
time: 94.8 us; the launch traced here: 94.6 us
  Pallas kernels  94.6 us (100%)
    pallas_call x1, Pallas kernels, lower_levels(): pl.pallas_call(functools.partial(contract_kernel, per), out_shape=jax.Sha...  88.5 us
    pallas_call x1, Pallas kernels, top_join(): pl.pallas_call(top_kernel, out_shape=jax.ShapeDtypeStruct((2, per, half,...  6.08 us

profile of v3, /device:TPU:13, one launch (start us, length us, event | category | flops | bytes accessed | tf_op | source)
XLA Modules:
  0.0 94.6 jit_solution(6685549767356873399)
XLA Ops:
  0.0 88.5 %lower_levels.1 = bf16[2,2,2,8,64,512]{5,4,3,2,1,0:T(8,128)(2,1)} custom-call(s32[7]{0:T(128)} %order_ref.3, bf16[4,2,2,512,512]{4,3,2,1,0:T(8,128)(2,1)} %leaves_ref.1), custom_call_target="tpu_custom_call" | custom-call | tf_op jit(solution)/shard_map/lower_levels/pallas_call | solution.py:316
  88.5 6.1 %top_join.1 = f32[2,2,256,512]{3,2,1,0:T(8,128)} custom-call(s32[7]{0:T(128)} %order_ref.3, s32[2]{0:T(128)} %slices_ref.1, bf16[2,2,2,512,512]{4,3,2,1,0:T(8,128)(2,1)} %bitcast.1, bf16[2,2,2,512,512]{4,3,2,1,0:T(8,128)(2,1)} %bitcast.2, bf16[2,2,512,512]{3,2,1,0:T(8,128)(2,1)} %chosen_ref.1), custom_call_target="tpu_custom_call" | custom-call | tf_op jit(solution)/shard_map/top_join/pallas_call | solution.py:369
